TPU v7x, 256 devices: a whole 4x4x8 slice. The times are simulated.
256 devices in a mesh: section: 8 (over x, z_hi), expert: 8 (over z_lo, core), tensor: 4 (over y).
Axes of the slice: x: 4, y: 4, z: 8 (z_hi: 2, z_lo: 4; z = z_hi * 4 + z_lo), core: 2. Of those that a mesh axis runs over, the one named last changes fastest.
Arguments:
- tokens: bfloat16 [512, 6144], P(('section', 'expert'), 'tensor'), may hold values from -6 to 6
- routes: int32 [512, 2], P(('section', 'expert')), may hold values from 0 to 7, all different within a row; in each aligned block of 8 rows (0 to 7, 8 to 15, ...) at most 4 rows name the same one
- router: float32 [6144, 8], replicated, may hold values from -0.18 to 0.18
- gate_proj: bfloat16 [8, 6144, 8192], P('expert', None, ('section', 'tensor')), may hold values from -0.078125 to 0.078125
- up_proj: bfloat16 [8, 6144, 8192], P('expert', None, ('section', 'tensor')), may hold values from -0.078125 to 0.078125
- down_proj: bfloat16 [8, 8192, 6144], P('expert', ('section', 'tensor')), may hold values from -0.125 to 0.125
- grad_out: bfloat16 [512, 6144], P(('section', 'expert'), 'tensor'), may hold values from -6 to 6
Outputs:
- moe_out: bfloat16 [512, 6144], P(('section', 'expert'), 'tensor')
- grad_tokens: bfloat16 [512, 6144], P(('section', 'expert'), 'tensor')
- grad_router: float32 [6144, 8], P('tensor')
Inputs may be any that keep to these rules, and one draw needn't show every extreme that they name: `routes`: each token names 2 different experts; in each aligned block of 8 tokens (the tokens of one group) no expert is named by more than 4 tokens, and in some blocks one expert is named by exactly 4.
All inputs are finite; a program needn't handle non-finite values.
Results may differ from a plain program's by a relative error of at most 0.02.
Values may be sent and summed in bfloat16 or wider, within the bound.
No kernel may reach another device: no remote copies, remote signals or barrier semaphores. Data moves between devices by JAX's collectives and lax.ppermute only.
A program may use at most 64 MiB of HBM per device.

v0:
```python
import jax
import jax.numpy as jnp
from jax import lax
from jax.sharding import PartitionSpec as P

precise = lax.Precision.HIGHEST


def route_table(routes, expert_count, capacity):
    flat_ids = routes.reshape(-1)
    expert_hot = (flat_ids[:, None] == jnp.arange(expert_count, dtype=jnp.int32)[None, :]).astype(
        jnp.float32
    )
    earlier = jnp.cumsum(expert_hot, axis=0) - expert_hot
    slot_ids = jnp.sum(earlier * expert_hot, axis=1).astype(jnp.int32)
    slot_hot = (slot_ids[:, None] == jnp.arange(capacity, dtype=jnp.int32)[None, :]).astype(
        jnp.float32
    )
    routing = expert_hot.T[:, None, :] * slot_hot.T[None, :, :]
    return routing.reshape(expert_count * capacity, flat_ids.shape[0])


def gate_weights(logits, routes):
    chosen = jnp.take_along_axis(logits, routes, axis=1)
    scores = jax.nn.sigmoid(chosen)
    totals = jnp.sum(scores, axis=1, keepdims=True)
    return (scores, scores / totals)


def expert_front(rows_x, gate_mat, up_mat):
    pre_gate = jnp.dot(rows_x, gate_mat, preferred_element_type=jnp.float32)
    pre_up = jnp.dot(rows_x, up_mat, preferred_element_type=jnp.float32)
    gate_sig = jax.nn.sigmoid(pre_gate)
    gate_act = pre_gate * gate_sig
    hidden = (gate_act * pre_up).astype(jnp.bfloat16)
    return (pre_gate, pre_up, gate_sig, gate_act, hidden)


def expert_grads(grad_hidden, pre_gate, pre_up, gate_sig, gate_act):
    grad_gate = (grad_hidden * pre_up * gate_sig * (1.0 + pre_gate * (1.0 - gate_sig))).astype(
        jnp.bfloat16
    )
    grad_up = (grad_hidden * gate_act).astype(jnp.bfloat16)
    return (grad_gate, grad_up)


def router_grads(grad_weight, scores, routes, expert_count):
    totals = scores[:, 0] + scores[:, 1]
    first = (grad_weight[:, 0] - grad_weight[:, 1]) * scores[:, 1] / (totals * totals)
    second = (grad_weight[:, 1] - grad_weight[:, 0]) * scores[:, 0] / (totals * totals)
    grad_scores = jnp.stack([first, second], axis=1)
    grad_chosen = grad_scores * scores * (1.0 - scores)
    expert_hot = (
        routes[:, :, None] == jnp.arange(expert_count, dtype=jnp.int32)[None, None, :]
    ).astype(jnp.float32)
    return jnp.sum(expert_hot * grad_chosen[:, :, None], axis=1)


def contract_last(left, right):
    return lax.dot_general(
        left, right, (((1,), (1,)), ((), ())), preferred_element_type=jnp.float32
    )


def on_device(tokens, routes, router, gate_proj, up_proj, down_proj, grad_out):
    tok_rows, quarter = tokens.shape
    tensor_count = lax.axis_size("tensor")
    expert_count = lax.axis_size("expert")
    top_count = routes.shape[1]
    capacity = 2 * tok_rows * top_count // expert_count
    block_rows = expert_count * capacity
    tensor_index = lax.axis_index("tensor")
    router_rows = lax.dynamic_slice_in_dim(router, tensor_index * quarter, quarter, 0)
    routing = route_table(routes, expert_count, capacity)
    gate_mat = gate_proj[0]
    up_mat = up_proj[0]
    down_mat = down_proj[0]
    send_x, send_dy = (tokens, grad_out)
    logits = lax.psum(jnp.dot(tokens.astype(jnp.float32), router_rows, precision=precise), "tensor")
    scores, weight = gate_weights(logits, routes)
    row_width = send_x.shape[1]
    x_sent = jnp.dot(
        routing, jnp.repeat(send_x.astype(jnp.float32), top_count, axis=0), precision=precise
    )
    x_sent = x_sent.astype(jnp.bfloat16).reshape(expert_count, capacity, row_width)
    scaled = jnp.repeat(send_dy.astype(jnp.float32), top_count, axis=0) * weight.reshape(-1, 1)
    dy_sent = (
        jnp.dot(routing, scaled, precision=precise)
        .astype(jnp.bfloat16)
        .reshape(expert_count, capacity, row_width)
    )

    def block_ids(count):
        return jnp.arange(count // block_rows, dtype=jnp.int32)

    def forward_block(hidden, block):
        section_at = block // tensor_count
        tensor_at = block % tensor_count
        hidden_rows = lax.dynamic_slice_in_dim(hidden, section_at * block_rows, block_rows, 0)
        columns = lax.dynamic_slice_in_dim(down_mat, tensor_at * quarter, quarter, 1)
        return jnp.dot(hidden_rows, columns, preferred_element_type=jnp.float32)

    def backward_block(grad_gate, grad_up, block):
        section_at = block // tensor_count
        tensor_at = block % tensor_count
        gate_rows = lax.dynamic_slice_in_dim(grad_gate, section_at * block_rows, block_rows, 0)
        up_rows = lax.dynamic_slice_in_dim(grad_up, section_at * block_rows, block_rows, 0)
        gate_part = lax.dynamic_slice_in_dim(gate_mat, tensor_at * quarter, quarter, 0)
        up_part = lax.dynamic_slice_in_dim(up_mat, tensor_at * quarter, quarter, 0)
        return contract_last(gate_rows, gate_part) + contract_last(up_rows, up_part)

    landed_x = lax.all_to_all(x_sent, "expert", split_axis=0, concat_axis=0, tiled=True)
    landed_x = lax.all_gather(landed_x, "tensor", axis=2, tiled=True)
    rows_x = lax.all_gather(landed_x.reshape(block_rows, -1), "section", axis=0, tiled=True)
    pre_gate, pre_up, gate_sig, gate_act, hidden = expert_front(rows_x, gate_mat, up_mat)
    summed_out = lax.psum_scatter(
        lax.map(
            lambda block: forward_block(hidden, block),
            block_ids(lax.axis_size(("section", "tensor")) * block_rows),
        )
        .reshape(lax.axis_size(("section", "tensor")) * block_rows, quarter)
        .astype(jnp.bfloat16),
        ("section", "tensor"),
        scatter_dimension=0,
        tiled=True,
    ).astype(jnp.float32)
    expert_out = lax.all_to_all(
        summed_out.reshape(expert_count, capacity, quarter).astype(jnp.bfloat16),
        "expert",
        split_axis=0,
        concat_axis=0,
        tiled=True,
    ).astype(jnp.float32)
    landed_dy = lax.all_to_all(dy_sent, "expert", split_axis=0, concat_axis=0, tiled=True)
    landed_dy = lax.all_gather(landed_dy, "tensor", axis=2, tiled=True)
    rows_dy = lax.all_gather(landed_dy.reshape(block_rows, -1), "section", axis=0, tiled=True)
    grad_hidden = contract_last(rows_dy, down_mat)
    grad_gate, grad_up = expert_grads(grad_hidden, pre_gate, pre_up, gate_sig, gate_act)
    summed_grad = lax.psum_scatter(
        lax.map(
            lambda block: backward_block(grad_gate, grad_up, block),
            block_ids(lax.axis_size(("section", "tensor")) * block_rows),
        )
        .reshape(lax.axis_size(("section", "tensor")) * block_rows, quarter)
        .astype(jnp.bfloat16),
        ("section", "tensor"),
        scatter_dimension=0,
        tiled=True,
    ).astype(jnp.float32)
    expert_grad = lax.all_to_all(
        summed_grad.reshape(expert_count, capacity, quarter).astype(jnp.bfloat16),
        "expert",
        split_axis=0,
        concat_axis=0,
        tiled=True,
    ).astype(jnp.float32)
    out_route = jnp.dot(
        routing.T, expert_out.reshape(block_rows, quarter), precision=precise
    ).reshape(tok_rows, top_count, quarter)
    grad_route = jnp.dot(
        routing.T, expert_grad.reshape(block_rows, quarter), precision=precise
    ).reshape(tok_rows, top_count, quarter)
    moe_out = jnp.sum(weight[:, :, None] * out_route, axis=1).astype(jnp.bfloat16)
    weight_part = jnp.sum(grad_out.astype(jnp.float32)[:, None, :] * out_route, axis=2)
    grad_weight = lax.psum(weight_part, "tensor")
    grad_logits = router_grads(grad_weight, scores, routes, expert_count)
    grad_tokens = (
        jnp.sum(grad_route, axis=1) + jnp.dot(grad_logits, router_rows.T, precision=precise)
    ).astype(jnp.bfloat16)
    router_part = jnp.dot(tokens.astype(jnp.float32).T, grad_logits, precision=precise)
    grad_router = lax.psum(router_part, ("section", "expert"))
    return (moe_out, grad_tokens, grad_router)


def solution(mesh):
    return jax.shard_map(
        on_device,
        mesh=mesh,
        in_specs=(
            P(("section", "expert"), "tensor"),
            P(("section", "expert"), None),
            P(),
            P("expert", None, ("section", "tensor")),
            P("expert", None, ("section", "tensor")),
            P("expert", ("section", "tensor"), None),
            P(("section", "expert"), "tensor"),
        ),
        out_specs=(
            P(("section", "expert"), "tensor"),
            P(("section", "expert"), "tensor"),
            P("tensor", None),
        ),
        check_vma=False,
    )
```

profile of v0, /device:TPU:8, one launch (start us, length us, event | category | flops | bytes accessed | tf_op | source)
XLA Modules:
  0.0 1154.4 jit_solution(11186698686855565210)
XLA Ops:
  9.6 12.0 %all_to_all.20 = bf16[8,4,1536]{2,1,0:T(4,128)(2,1)S(1)} all-to-all(bf16[8,4,1536]{2,1,0:T(4,128)(2,1)S(1)} %reshape.192), channel_id=1, replica_groups=mesh['section'=8,'expert'=8,'tensor'=4] {'expert'}, dimensions={0} | all-to-all | bytes 196608 | tf_op jit(solution)/shard_map/all_to_all | solution.py:112
  21.7 13.1 %all_gather.12 = bf16[8,4,6144]{2,1,0:T(4,128)(2,1)S(1)} all-gather(bf16[8,4,1536]{2,1,0:T(4,128)(2,1)S(1)} %all_to_all.20), channel_id=1, replica_groups=mesh['section'=8,'expert'=8,'tensor'=4] {'tensor'}, dimensions={2}, use_global_device_ids=true | all-gather | bytes 491520 | tf_op jit(solution)/shard_map/all_gather | solution.py:113
  37.5 8.1 psum.21
  47.0 16.7 %all_to_all.21 = bf16[8,4,1536]{2,1,0:T(4,128)(2,1)S(1)} all-to-all(bf16[8,4,1536]{2,1,0:T(4,128)(2,1)S(1)} %reshape.195), channel_id=1, replica_groups=mesh['section'=8,'expert'=8,'tensor'=4] {'expert'}, dimensions={0} | all-to-all | bytes 196608 | tf_op jit(solution)/shard_map/all_to_all | solution.py:134
  63.7 12.4 %all_gather.14 = bf16[8,4,6144]{2,1,0:T(4,128)(2,1)S(1)} all-gather(bf16[8,4,1536]{2,1,0:T(4,128)(2,1)S(1)} %all_to_all.21), channel_id=1, replica_groups=mesh['section'=8,'expert'=8,'tensor'=4] {'tensor'}, dimensions={2}, use_global_device_ids=true | all-gather | bytes 491520 | tf_op jit(solution)/shard_map/all_gather | solution.py:135
  77.1 51.9 %all-gather.3.cloned.1.call-done = bf16[256,6144]{1,0:T(8,128)(2,1)} async-done(((bf16[32,6144]{1,0:T(8,128)(2,1)}), bf16[256,6144]{1,0:T(8,128)(2,1)}) %all-gather.3.cloned.1.call-update) | async-done | bytes 3145744 | tf_op jit(solution)/shard_map/all_gather | solution.py:114
  129.0 4.7 fusion.29
  133.7 1.7 fusion.31
  135.4 83.3 %all-gather.5.cloned.1.call-done = bf16[256,6144]{1,0:T(8,128)(2,1)} async-done(((bf16[32,6144]{1,0:T(8,128)(2,1)}), bf16[256,6144]{1,0:T(8,128)(2,1)}) %all-gather.5.cloned.1.call-update) | async-done | bytes 3145744 | tf_op jit(solution)/shard_map/all_gather | solution.py:136
  218.7 4.6 multiply_convert_fusion
  223.7 147.5 %while.24 = (s32[]{:T(128)}, bf16[32,32,1536]{2,1,0:T(8,128)(2,1)S(1)}, s32[32]{0:T(128)S(1)}, bf16[256,256]{1,0:T(8,128)(2,1)}, bf16[256,6144]{1,0:T(8,128)(2,1...) while((s32[]{:T(128)}, ...), condition=%wide.region_5.6_spmd, body=%wide.region_4.5_spmd.sunk | while | flops 25165852 | bytes 999876 | solution.py:117
  371.1 1.7 copy-done.2
  373.2 198.6 %while.25 = (s32[]{:T(128)}, bf16[32,32,1536]{2,1,0:T(8,128)(2,1)S(1)}, s32[32]{0:T(128)S(1)}, bf16[256,256]{1,0:T(8,128)(2,1)}, bf16[6144,256]{1,0:T(8,128)(2,1...) while((s32[]{:T(128)}, ...), condition=%wide.region_9.10_spmd, body=%wide.region_8.9_spmd.sunk | while | flops 50380828 | bytes 2195932 | solution.py:140
  396.6 1.5 fusion.64
  409.0 1.5 fusion.64
  421.4 1.5 fusion.64
  433.8 1.5 fusion.64
  446.2 1.5 fusion.64
  457.2 1.5 fusion.63
  458.7 1.5 fusion.64
  477.3 1.5 fusion.64
  483.5 1.5 fusion.64
  495.9 1.5 fusion.64
  571.9 1.7 copy-done.1
  573.6 52.4 %reduce-scatter.3.cloned.1.call-done = bf16[32,1536]{1,0:T(8,128)(2,1)} async-done(((bf16[1024,1536]{1,0:T(8,128)(2,1)}), bf16[32,1536]{1,0:T(8,128)(2,1)}) %reduce-scatter.3.cloned.1.call-update) | async-done | bytes 98320 | tf_op jit(solution)/shard_map/reduce_scatter | solution.py:116
  626.0 1.5 convert_element_type.89
  627.5 3.4 all-to-all-start.1
  631.0 253.9 %reduce-scatter.5.cloned.1.call-done = bf16[32,1536]{1,0:T(8,128)(2,1)} async-done(((bf16[1024,1536]{1,0:T(8,128)(2,1)}), bf16[32,1536]{1,0:T(8,128)(2,1)}) %reduce-scatter.5.cloned.1.call-update) | async-done | bytes 98320 | tf_op jit(solution)/shard_map/reduce_scatter | solution.py:139
  884.9 1.6 convert_element_type.97
  886.4 3.4 all-to-all-start.3
  890.6 9.5 psum.22
  900.4 246.4 %psum.23 = f32[1536,8]{0,1:T(8,128)} all-reduce(f32[1536,8]{0,1:T(8,128)S(1)} %convolution_bitcast_fusion.1), channel_id=1, replica_groups=mesh['section'=8,'expert'=8,'tensor'=4] {'section','expert'}, use_global_device_ids=true, to_apply=%region_15.16 | all-reduce | flops 12288 | bytes 98304 | tf_op jit(solution)/shard_map/psum | solution.py:171
  (218 shorter events, 172.9 us)
Async XLA Ops:
  7.2 29.4 %copy-start = (f32[6144,8]{0,1:T(8,128)S(1)}, f32[6144,8]{0,1:T(8,128)}, u32[]{:S(2)}) copy-start(f32[6144,8]{0,1:T(8,128)} %param.13) | copy-start | bytes 589828
  7.2 121.8 %all-gather.3.cloned.1.call-start = ((), (), s32[]{:S(2)}) async-start(), calls=%async_computation.6 | async-start | bytes 3538944 | tf_op jit(solution)/shard_map/all_gather | solution.py:114
  9.6 36.7 %copy-start.5 = (bf16[8,1536]{1,0:T(8,128)(2,1)S(1)}, bf16[8,1536]{1,0:T(8,128)(2,1)}, u32[]{:S(2)}) copy-start(bf16[8,1536]{1,0:T(8,128)(2,1)} %param.17) | copy-start | bytes 73732
  9.6 36.7 %copy-start.6 = (s32[8,2]{0,1:T(2,128)S(1)}, s32[8,2]{0,1:T(2,128)}, u32[]{:S(2)}) copy-start(s32[8,2]{0,1:T(2,128)} %param.12) | copy-start | bytes 196
  35.7 183.0 %all-gather.5.cloned.1.call-start = ((), (), s32[]{:S(2)}) async-start(), calls=%async_computation.8 | async-start | bytes 3538944 | tf_op jit(solution)/shard_map/all_gather | solution.py:136
  77.0 549.0 %reduce-scatter.3.cloned.1.call-start = ((), (), s32[]{:S(2)}) async-start(), calls=%async_computation.7 | async-start | bytes 3244032 | tf_op jit(solution)/shard_map/reduce_scatter | solution.py:116
  77.0 56.6 %copy-start.3 = (bf16[1,6144,256]{2,1,0:T(8,128)(2,1)S(1)}, bf16[1,6144,256]{2,1,0:T(8,128)(2,1)}, u32[]{:S(2)}) copy-start(bf16[1,6144,256]{2,1,0:T(8,128)(2,1)} %param.14) | copy-start | bytes 9437188
  129.0 4.7 copy-start.7
  371.1 1.7 copy-start.2
  372.8 512.0 %reduce-scatter.5.cloned.1.call-start = ((), (), s32[]{:S(2)}) async-start(), calls=%async_computation.9 | async-start | bytes 3244032 | tf_op jit(solution)/shard_map/reduce_scatter | solution.py:139
  571.9 1.7 copy-start.1
  571.9 328.3 %copy-start.4 = (bf16[8,1536]{1,0:T(8,128)(2,1)S(1)}, bf16[8,1536]{1,0:T(8,128)(2,1)}, u32[]{:S(2)}) copy-start(bf16[8,1536]{1,0:T(8,128)(2,1)} %param.11) | copy-start | bytes 73732
  627.5 258.9 %all-to-all-start.1 = ((bf16[8,4,1536]{2,1,0:T(4,128)(2,1)}), bf16[8,4,1536]{2,1,0:T(4,128)(2,1)S(1)}, u32[]{:S(2)}, u32[]{:S(2)}) async-start(bf16[8,4,1536]{2,1,0:T(4,128)(2,1)} %convert_element_type.89), calls=%async_computation.2 | async-start | bytes 196608 | tf_op jit(solution)/shard_map/all_to_all | solution.py:127
  886.4 260.4 %all-to-all-start.3 = ((bf16[8,4,1536]{2,1,0:T(4,128)(2,1)}), bf16[8,4,1536]{2,1,0:T(4,128)(2,1)S(1)}, u32[]{:S(2)}, u32[]{:S(2)}) async-start(bf16[8,4,1536]{2,1,0:T(4,128)(2,1)} %convert_element_type.97), calls=%async_computation.5 | async-start | bytes 196608 | tf_op jit(solution)/shard_map/all_to_all | solution.py:150
Sparse Core Ops, SparseCore 0:
  35.8 93.1 all-gather.2
  131.6 87.0 all-gather.4
  373.0 252.9 reduce-scatter.2
  632.1 252.7 reduce-scatter.4
where the time goes:
time: 1160 us; the launch traced here: 1150 us
  waiting for transfers between devices  442 us (38%)
  blocking collectives  318 us (27%)
  loops' own time  169 us (15%)
  matrix products  154 us (13%)
  local copies, waits for them, and re-layouts  50 us (4%)
  between operations  14 us (1%)
    reduce_scatter x1, waiting for transfers between devices, on_device(): lax.psum_scatter(lax.map(lambda block: backward_block(grad_gate, grad_up,...  254 us
    psum x1, blocking collectives, on_device(): grad_router = lax.psum(router_part, ('section', 'expert'))  246 us
    dot_general x65, matrix products, contract_last(): lax.dot_general(left, right, (((1,), (1,)), ((), ())), preferred_element_...  99.8 us
    another operation x1, loops' own time, on_device(): lax.map(lambda block: backward_block(grad_gate, grad_up, block), block_id...  84.7 us
    another operation x1, loops' own time, on_device(): lax.map(lambda block: forward_block(hidden, block), block_ids(lax.axis_si...  83.9 us
    all_gather x1, waiting for transfers between devices, on_device(): lax.all_gather(landed_dy.reshape(block_rows, -1), 'section', axis=0, tile...  83.3 us
    reduce_scatter x1, waiting for transfers between devices, on_device(): lax.psum_scatter(lax.map(lambda block: forward_block(hidden, block), bloc...  52.4 us
    all_gather x1, waiting for transfers between devices, on_device(): lax.all_gather(landed_x.reshape(block_rows, -1), 'section', axis=0, tiled...  51.9 us
  transfers between devices with their start and end apart: 6, of which 4 were waited for; matrix products, arithmetic and copies ran while one was open for 11% of the time, Pallas kernels for 0%

commit v1 on v0

--- a/solution.py
+++ b/solution.py
@@ -168,7 +168,7 @@
         jnp.sum(grad_route, axis=1) + jnp.dot(grad_logits, router_rows.T, precision=precise)
     ).astype(jnp.bfloat16)
     router_part = jnp.dot(tokens.astype(jnp.float32).T, grad_logits, precision=precise)
-    grad_router = lax.psum(router_part, ("section", "expert"))
+    grad_router = lax.psum(lax.psum(router_part, "section"), "expert")
     return (moe_out, grad_tokens, grad_router)
 
 

time: 1160 us -> 993 us (0.86)
  blocking collectives: 318 us -> 148 us
    psum x1 -> x2, blocking collectives: 246 us -> 76.2 us  [on_device(): grad_router = lax.psum(lax.psum(router_part, 'section'), 'expert')]
  transfers between devices with their start and end apart: 6 -> 6, of which waited for: 4 -> 4; matrix products, arithmetic and copies ran while one was open for 11% -> 13% of each run, Pallas kernels for 0% -> 0%
where the time goes in v1:
time: 993 us; the launch traced here: 984 us
  waiting for transfers between devices  442 us (45%)
  loops' own time  169 us (17%)
  matrix products  154 us (16%)
  blocking collectives  148 us (15%)
  local copies, waits for them, and re-layouts  50 us (5%)
  between operations  14 us (1%)
    reduce_scatter x1, waiting for transfers between devices, on_device(): lax.psum_scatter(lax.map(lambda block: backward_block(grad_gate, grad_up,...  254 us
    dot_general x65, matrix products, contract_last(): lax.dot_general(left, right, (((1,), (1,)), ((), ())), preferred_element_...  99.8 us
    another operation x1, loops' own time, on_device(): lax.map(lambda block: backward_block(grad_gate, grad_up, block), block_id...  84.7 us
    another operation x1, loops' own time, on_device(): lax.map(lambda block: forward_block(hidden, block), block_ids(lax.axis_si...  83.9 us
    all_gather x1, waiting for transfers between devices, on_device(): lax.all_gather(landed_dy.reshape(block_rows, -1), 'section', axis=0, tile...  83.3 us
    psum x2, blocking collectives, on_device(): grad_router = lax.psum(lax.psum(router_part, 'section'), 'expert')  76.2 us
    reduce_scatter x1, waiting for transfers between devices, on_device(): lax.psum_scatter(lax.map(lambda block: forward_block(hidden, block), bloc...  52.4 us
    all_gather x1, waiting for transfers between devices, on_device(): lax.all_gather(landed_x.reshape(block_rows, -1), 'section', axis=0, tiled...  51.9 us
  transfers between devices with their start and end apart: 6, of which 4 were waited for; matrix products, arithmetic and copies ran while one was open for 13% of the time, Pallas kernels for 0%

profile of v1, /device:TPU:8, one launch (start us, length us, event | category | flops | bytes accessed | tf_op | source)
XLA Modules:
  0.0 984.1 jit_solution(16698983691617334665)
XLA Ops:
  9.6 12.0 %all_to_all.20 = bf16[8,4,1536]{2,1,0:T(4,128)(2,1)S(1)} all-to-all(bf16[8,4,1536]{2,1,0:T(4,128)(2,1)S(1)} %reshape.192), channel_id=1, replica_groups=mesh['section'=8,'expert'=8,'tensor'=4] {'expert'}, dimensions={0} | all-to-all | bytes 196608 | tf_op jit(solution)/shard_map/all_to_all | solution.py:112
  21.7 13.1 %all_gather.12 = bf16[8,4,6144]{2,1,0:T(4,128)(2,1)S(1)} all-gather(bf16[8,4,1536]{2,1,0:T(4,128)(2,1)S(1)} %all_to_all.20), channel_id=1, replica_groups=mesh['section'=8,'expert'=8,'tensor'=4] {'tensor'}, dimensions={2}, use_global_device_ids=true | all-gather | bytes 491520 | tf_op jit(solution)/shard_map/all_gather | solution.py:113
  37.5 8.1 psum.28
  47.0 16.7 %all_to_all.21 = bf16[8,4,1536]{2,1,0:T(4,128)(2,1)S(1)} all-to-all(bf16[8,4,1536]{2,1,0:T(4,128)(2,1)S(1)} %reshape.195), channel_id=1, replica_groups=mesh['section'=8,'expert'=8,'tensor'=4] {'expert'}, dimensions={0} | all-to-all | bytes 196608 | tf_op jit(solution)/shard_map/all_to_all | solution.py:134
  63.7 12.4 %all_gather.14 = bf16[8,4,6144]{2,1,0:T(4,128)(2,1)S(1)} all-gather(bf16[8,4,1536]{2,1,0:T(4,128)(2,1)S(1)} %all_to_all.21), channel_id=1, replica_groups=mesh['section'=8,'expert'=8,'tensor'=4] {'tensor'}, dimensions={2}, use_global_device_ids=true | all-gather | bytes 491520 | tf_op jit(solution)/shard_map/all_gather | solution.py:135
  77.1 51.9 %all-gather.3.cloned.1.call-done = bf16[256,6144]{1,0:T(8,128)(2,1)} async-done(((bf16[32,6144]{1,0:T(8,128)(2,1)}), bf16[256,6144]{1,0:T(8,128)(2,1)}) %all-gather.3.cloned.1.call-update) | async-done | bytes 3145744 | tf_op jit(solution)/shard_map/all_gather | solution.py:114
  129.0 4.7 fusion.29
  133.7 1.7 fusion.31
  135.4 83.3 %all-gather.5.cloned.1.call-done = bf16[256,6144]{1,0:T(8,128)(2,1)} async-done(((bf16[32,6144]{1,0:T(8,128)(2,1)}), bf16[256,6144]{1,0:T(8,128)(2,1)}) %all-gather.5.cloned.1.call-update) | async-done | bytes 3145744 | tf_op jit(solution)/shard_map/all_gather | solution.py:136
  218.7 4.6 multiply_convert_fusion
  223.7 147.5 %while.24 = (s32[]{:T(128)}, bf16[32,32,1536]{2,1,0:T(8,128)(2,1)S(1)}, s32[32]{0:T(128)S(1)}, bf16[256,256]{1,0:T(8,128)(2,1)}, bf16[256,6144]{1,0:T(8,128)(2,1...) while((s32[]{:T(128)}, ...), condition=%wide.region_5.6_spmd, body=%wide.region_4.5_spmd.sunk | while | flops 25165852 | bytes 999876 | solution.py:117
  371.1 1.7 copy-done.2
  373.2 198.6 %while.25 = (s32[]{:T(128)}, bf16[32,32,1536]{2,1,0:T(8,128)(2,1)S(1)}, s32[32]{0:T(128)S(1)}, bf16[256,256]{1,0:T(8,128)(2,1)}, bf16[6144,256]{1,0:T(8,128)(2,1...) while((s32[]{:T(128)}, ...), condition=%wide.region_9.10_spmd, body=%wide.region_8.9_spmd.sunk | while | flops 50380828 | bytes 2195932 | solution.py:140
  396.6 1.5 fusion.64
  409.0 1.5 fusion.64
  421.4 1.5 fusion.64
  433.8 1.5 fusion.64
  446.2 1.5 fusion.64
  457.2 1.5 fusion.63
  458.7 1.5 fusion.64
  477.3 1.5 fusion.64
  483.5 1.5 fusion.64
  571.9 1.7 copy-done.1
  573.6 52.4 %reduce-scatter.3.cloned.1.call-done = bf16[32,1536]{1,0:T(8,128)(2,1)} async-done(((bf16[1024,1536]{1,0:T(8,128)(2,1)}), bf16[32,1536]{1,0:T(8,128)(2,1)}) %reduce-scatter.3.cloned.1.call-update) | async-done | bytes 98320 | tf_op jit(solution)/shard_map/reduce_scatter | solution.py:116
  626.0 1.5 convert_element_type.89
  627.5 3.4 all-to-all-start.1
  631.0 253.9 %reduce-scatter.5.cloned.1.call-done = bf16[32,1536]{1,0:T(8,128)(2,1)} async-done(((bf16[1024,1536]{1,0:T(8,128)(2,1)}), bf16[32,1536]{1,0:T(8,128)(2,1)}) %reduce-scatter.5.cloned.1.call-update) | async-done | bytes 98320 | tf_op jit(solution)/shard_map/reduce_scatter | solution.py:139
  884.9 1.6 convert_element_type.97
  886.4 3.4 all-to-all-start.3
  890.6 9.5 psum.29
  900.4 49.1 %psum.30 = f32[1536,8]{0,1:T(8,128)S(1)} all-reduce(f32[1536,8]{0,1:T(8,128)S(1)} %convolution_bitcast_fusion.1), channel_id=1, replica_groups=mesh['section'=8,'expert'=8,'tensor'=4] {'section'}, use_global_device_ids=true, to_apply=%region_15.16 | all-reduce | flops 12288 | bytes 98304 | tf_op jit(solution)/shard_map/psum | solution.py:171
  949.5 27.1 %psum.31 = f32[1536,8]{0,1:T(8,128)} all-reduce(f32[1536,8]{0,1:T(8,128)S(1)} %psum.30), channel_id=1, replica_groups=mesh['section'=8,'expert'=8,'tensor'=4] {'expert'}, use_global_device_ids=true, to_apply=%region_16.17 | all-reduce | flops 12288 | bytes 98304 | tf_op jit(solution)/shard_map/psum | solution.py:171
  (219 shorter events, 174.4 us)
Async XLA Ops:
  7.2 29.4 %copy-start = (f32[6144,8]{0,1:T(8,128)S(1)}, f32[6144,8]{0,1:T(8,128)}, u32[]{:S(2)}) copy-start(f32[6144,8]{0,1:T(8,128)} %param.13) | copy-start | bytes 589828
  7.2 121.8 %all-gather.3.cloned.1.call-start = ((), (), s32[]{:S(2)}) async-start(), calls=%async_computation.6 | async-start | bytes 3538944 | tf_op jit(solution)/shard_map/all_gather | solution.py:114
  9.6 36.7 %copy-start.5 = (bf16[8,1536]{1,0:T(8,128)(2,1)S(1)}, bf16[8,1536]{1,0:T(8,128)(2,1)}, u32[]{:S(2)}) copy-start(bf16[8,1536]{1,0:T(8,128)(2,1)} %param.17) | copy-start | bytes 73732
  9.6 36.7 %copy-start.6 = (s32[8,2]{0,1:T(2,128)S(1)}, s32[8,2]{0,1:T(2,128)}, u32[]{:S(2)}) copy-start(s32[8,2]{0,1:T(2,128)} %param.12) | copy-start | bytes 196
  35.7 183.0 %all-gather.5.cloned.1.call-start = ((), (), s32[]{:S(2)}) async-start(), calls=%async_computation.8 | async-start | bytes 3538944 | tf_op jit(solution)/shard_map/all_gather | solution.py:136
  77.0 549.0 %reduce-scatter.3.cloned.1.call-start = ((), (), s32[]{:S(2)}) async-start(), calls=%async_computation.7 | async-start | bytes 3244032 | tf_op jit(solution)/shard_map/reduce_scatter | solution.py:116
  77.0 56.6 %copy-start.3 = (bf16[1,6144,256]{2,1,0:T(8,128)(2,1)S(1)}, bf16[1,6144,256]{2,1,0:T(8,128)(2,1)}, u32[]{:S(2)}) copy-start(bf16[1,6144,256]{2,1,0:T(8,128)(2,1)} %param.14) | copy-start | bytes 9437188
  129.0 4.7 copy-start.7
  371.1 1.7 copy-start.2
  372.8 512.0 %reduce-scatter.5.cloned.1.call-start = ((), (), s32[]{:S(2)}) async-start(), calls=%async_computation.9 | async-start | bytes 3244032 | tf_op jit(solution)/shard_map/reduce_scatter | solution.py:139
  571.9 1.7 copy-start.1
  571.9 328.3 %copy-start.4 = (bf16[8,1536]{1,0:T(8,128)(2,1)S(1)}, bf16[8,1536]{1,0:T(8,128)(2,1)}, u32[]{:S(2)}) copy-start(bf16[8,1536]{1,0:T(8,128)(2,1)} %param.11) | copy-start | bytes 73732
  627.5 258.9 %all-to-all-start.1 = ((bf16[8,4,1536]{2,1,0:T(4,128)(2,1)}), bf16[8,4,1536]{2,1,0:T(4,128)(2,1)S(1)}, u32[]{:S(2)}, u32[]{:S(2)}) async-start(bf16[8,4,1536]{2,1,0:T(4,128)(2,1)} %convert_element_type.89), calls=%async_computation.2 | async-start | bytes 196608 | tf_op jit(solution)/shard_map/all_to_all | solution.py:127
  886.4 90.2 %all-to-all-start.3 = ((bf16[8,4,1536]{2,1,0:T(4,128)(2,1)}), bf16[8,4,1536]{2,1,0:T(4,128)(2,1)S(1)}, u32[]{:S(2)}, u32[]{:S(2)}) async-start(bf16[8,4,1536]{2,1,0:T(4,128)(2,1)} %convert_element_type.97), calls=%async_computation.5 | async-start | bytes 196608 | tf_op jit(solution)/shard_map/all_to_all | solution.py:150
Sparse Core Ops, SparseCore 0:
  35.8 93.1 all-gather.2
  131.6 87.0 all-gather.4
  373.0 252.9 reduce-scatter.2
  632.1 252.7 reduce-scatter.4
